TPU v7x, 512 devices: a whole 4x8x8 slice. The times are simulated.
512 devices in a mesh: phi: 8 (over z), theta: 16 (over y, core), row: 4 (over x).
Axes of the slice: x: 4, y: 8, z: 8, core: 2. Of those that a mesh axis runs over, the one named last changes fastest.
Arguments:
- fields: float32 [8, 12, 1536, 2048], P(None, 'row', 'phi', 'theta'), may hold values from -6 to 6
- kept_counts: int32 [512], replicated, may hold values from 1 to 384, as said below
Outputs:
- filtered: float32 [8, 12, 1536, 2048], P(None, 'row', 'phi', 'theta')
Inputs may be any that keep to these rules, and one draw needn't show every extreme that they name: `kept_counts`: modes 0 to count - 1 of a cap row are kept; some row reaches 384 in every draw.
All inputs are finite; a program needn't handle non-finite values.
Results may differ from a plain program's by a relative error of at most 0.00007.
Values sent between devices are 32-bit elements; how exact they have to be, the bound alone decides.
No kernel may reach another device: no remote copies, remote signals or barrier semaphores. Data moves between devices by JAX's collectives and lax.ppermute only.
A program may use at most 64 MiB of HBM per device.

v0:
```python
import math
import jax
import jax.numpy as jnp
from jax import lax
from jax.sharding import PartitionSpec as P

KMAX = 384


def tables(offset, span_rows, points, mode_count):
    azimuth = offset + jnp.arange(span_rows, dtype=jnp.int32)
    wavenumber = jnp.arange(mode_count, dtype=jnp.int32)
    phase_turns = azimuth[:, None] * wavenumber[None, :] % points
    angles = phase_turns.astype(jnp.float32) * (2.0 * math.pi / points)
    forward = jnp.concatenate([jnp.cos(angles), jnp.sin(angles)], axis=1)
    weight = jnp.where(wavenumber == 0, 1.0, 2.0).astype(jnp.float32) / points
    weight = jnp.concatenate([weight, weight])
    backward = (forward * weight[None, :]).T
    return (forward, backward)


def spectral(lines, row_counts):
    nfields, shells, local_points, rows_here = lines.shape
    n_phi = lax.axis_size("phi")
    points = local_points * n_phi
    highest = lax.Precision.HIGHEST
    groups = nfields * shells
    grouped = lines.reshape(groups, local_points, rows_here)
    line_counts = jnp.broadcast_to(row_counts[None, :], (groups, rows_here)).reshape(-1)
    phi_index = lax.axis_index("phi")
    forward, backward = tables(phi_index * local_points, local_points, points, KMAX)
    share_rows = forward.shape[1] // n_phi
    out = jnp.einsum(
        "pk,gpr->kgr", forward, grouped, precision=highest, preferred_element_type=jnp.float32
    )
    share = lax.psum_scatter(
        out.reshape(share_rows * lax.axis_size("phi"), groups * rows_here),
        "phi",
        scatter_dimension=0,
        tiled=True,
    )
    share_index = phi_index * share_rows + jnp.arange(share_rows, dtype=jnp.int32)
    keep = (share_index % KMAX)[:, None] < line_counts[None, :]
    masked = jnp.where(keep, share, 0.0)
    piece = lax.all_gather(masked, "phi", axis=0, tiled=True)
    stacked = piece.reshape(piece.shape[0], groups, rows_here)
    result = jnp.einsum(
        "kp,kgr->gpr", backward, stacked, precision=highest, preferred_element_type=jnp.float32
    )
    return result.reshape(lines.shape)


def on_device(fields, kept_counts):
    n_theta = lax.axis_size("theta")
    theta_index = lax.axis_index("theta")
    band_rows = fields.shape[3]
    caps = kept_counts.shape[0] // band_rows
    cap_bands = caps // 2
    count_table = kept_counts.reshape(caps, band_rows)
    piece_rows = band_rows // n_theta
    received = lax.all_to_all(fields, "theta", split_axis=3, concat_axis=3, tiled=True)
    north_end = cap_bands * piece_rows
    south_start = (n_theta - cap_bands) * piece_rows
    cap_lines = jnp.concatenate(
        [received[:, :, :, :north_end], received[:, :, :, south_start:]], axis=3
    )
    row_counts = lax.dynamic_slice_in_dim(
        count_table, theta_index * piece_rows, piece_rows, 1
    ).reshape(-1)
    smoothed = spectral(cap_lines, row_counts)
    rebuilt = jnp.concatenate(
        [
            smoothed[:, :, :, :north_end],
            received[:, :, :, north_end:south_start],
            smoothed[:, :, :, north_end:],
        ],
        axis=3,
    )
    return lax.all_to_all(rebuilt, "theta", split_axis=3, concat_axis=3, tiled=True)


def solution(mesh):
    placed = (P(None, "row", "phi", "theta"), P())
    return jax.shard_map(
        on_device,
        mesh=mesh,
        in_specs=placed,
        out_specs=P(None, "row", "phi", "theta"),
        check_vma=False,
    )
```

profile of v0, /device:TPU:1, one launch (start us, length us, event | category | flops | bytes accessed | tf_op | source)
XLA Modules:
  0.0 286.2 jit_solution(12094316669807166460)
XLA Ops:
  6.5 0.0 copy-start
  6.5 3.6 %copy.26 = f32[8,3,192,128]{2,0,1,3:T(8,128)} copy(f32[8,3,192,128]{3,2,1,0:T(8,128)} %param.2) | data formatting | bytes 4718592 | tf_op args[0]
  10.1 10.4 %all-to-all-start = ((f32[8,3,192,128]{2,0,1,3:T(8,128)}), f32[8,3,192,128]{2,0,1,3:T(8,128)S(1)}, u32[]{:S(2)}, u32[]{:S(2)}) async-start(f32[8,3,192,128]{2,0,1,3:T(8,128)} %copy.26), calls=%async_computation | async-start | bytes 6291456 | tf_op jit(solution)/shard_map/all_to_all | solution.py:61
  20.5 0.0 reduce-scatter.2.cloned.1.call-start
  20.5 2.1 fusion.10
  22.6 68.9 %all-to-all-done = f32[8,3,192,128]{2,0,1,3:T(8,128)S(1)} async-done(((f32[8,3,192,128]{2,0,1,3:T(8,128)}), f32[8,3,192,128]{2,0,1,3:T(8,128)S(1)}, u32[]{:S(2)}, u32[]{:S(2)}) %all-to-all-start) | async-done | bytes 2359328 | tf_op jit(solution)/shard_map/all_to_all | solution.py:61
  91.5 0.0 copy-start.1
  91.5 0.0 copy-start.2
  91.5 0.1 fusion.14
  91.5 0.1 copy.27
  91.7 0.1 copy.28
  91.8 0.1 pad_maximum_fusion.1
  91.9 0.7 copy-done.2
  92.6 5.4 %fusion.3 = f32[768,768]{1,0:T(8,128)} fusion(f32[768,192]{1,0:T(8,128)S(1)} %bitcast.17, f32[192,384]{1,0:T(8,128)S(1)} %copy-done.2, f32[192,384]{1,0:T(8,128)S(1)} %get-tuple-element.9), kind=kOutput, calls=%fused_computation.6 | convolution fusion | flops 1359101952 | bytes 3538944 | tf_op jit(solution)/shard_map/pk,gpr->kgr/dot_general | solution.py:33
  98.0 0.0 reduce-scatter.2.cloned.1.call-update
  98.0 0.0 all-gather.2.cloned.1.call-start
  98.1 0.0 copy-done
  98.1 0.1 constant_dynamic-slice_fusion
  98.1 0.1 broadcast_in_dim.23
  98.2 0.1 lt.33
  98.3 42.2 %reduce-scatter.2.cloned.1.call-done = f32[96,768]{1,0:T(8,128)} async-done(((f32[768,768]{1,0:T(8,128)}), f32[96,768]{1,0:T(8,128)}) %reduce-scatter.2.cloned.1.call-update) | async-done | bytes 294928 | tf_op jit(solution)/shard_map/reduce_scatter | solution.py:36
  140.5 1.8 compare_select_fusion
  142.2 0.0 all-gather.2.cloned.1.call-update
  142.3 0.0 copy-done.1
  142.3 0.0 copy-start.3
  142.3 44.4 %all-gather.2.cloned.1.call-done = f32[768,768]{1,0:T(8,128)} async-done(((f32[96,768]{1,0:T(8,128)}), f32[768,768]{1,0:T(8,128)}) %all-gather.2.cloned.1.call-update) | async-done | bytes 2359312 | tf_op jit(solution)/shard_map/all_gather | solution.py:45
  186.7 2.0 copy.29
  188.8 0.0 copy-done.3
  188.8 2.0 fusion
  190.8 0.0 slice-start
  190.8 0.1 fusion.15
  190.9 0.2 copy.33
  191.1 0.2 copy.34
  191.4 1.1 slice-done
  192.5 0.2 pad_maximum_fusion
  192.7 84.5 %all_to_all.10 = f32[8,3,192,128]{2,0,1,3:T(8,128)S(1)} all-to-all(f32[8,3,192,128]{2,0,1,3:T(8,128)S(1)} %pad_maximum_fusion), channel_id=1, replica_groups=mesh['phi'=8,'theta'=16,'row'=4] {'theta'}, dimensions={3} | all-to-all | bytes 4718592 | tf_op jit(solution)/shard_map/all_to_all | solution.py:79
  277.2 2.1 copy.32
  (5 shorter events, 0.0 us)
Async XLA Ops:
  6.5 91.5 %copy-start = (s32[512]{0:T(512)S(1)}, s32[512]{0:T(512)}, u32[]{:S(2)}) copy-start(s32[512]{0:T(512)} %param.3) | copy-start | bytes 6148
  10.1 81.4 %all-to-all-start = ((f32[8,3,192,128]{2,0,1,3:T(8,128)}), f32[8,3,192,128]{2,0,1,3:T(8,128)S(1)}, u32[]{:S(2)}, u32[]{:S(2)}) async-start(f32[8,3,192,128]{2,0,1,3:T(8,128)} %copy.26), calls=%async_computation | async-start | bytes 6291456 | tf_op jit(solution)/shard_map/all_to_all | solution.py:61
  20.5 120.0 %reduce-scatter.2.cloned.1.call-start = ((), (), s32[]{:S(2)}) async-start(), calls=%async_computation.3 | async-start | bytes 2654208 | tf_op jit(solution)/shard_map/reduce_scatter | solution.py:36
  91.5 50.8 %copy-start.1 = (f32[8,3,192,128]{2,0,1,3:T(8,128)}, f32[8,3,192,128]{2,0,1,3:T(8,128)S(1)}, u32[]{:S(2)}) copy-start(f32[8,3,192,128]{2,0,1,3:T(8,128)S(1)} %all-to-all-done) | copy-start | bytes 7077892
  91.5 1.2 copy-start.2
  98.0 88.7 %all-gather.2.cloned.1.call-start = ((), (), s32[]{:S(2)}) async-start(), calls=%async_computation.4 | async-start | bytes 2654208 | tf_op jit(solution)/shard_map/all_gather | solution.py:45
  142.3 46.5 %copy-start.3 = (f32[192,384]{1,0:T(8,128)S(1)}, f32[192,384]{1,0:T(8,128)}, u32[]{:S(2)}) copy-start(f32[192,384]{1,0:T(8,128)} %get-tuple-element.10) | copy-start | bytes 884740
  190.8 1.7 slice-start
Sparse Core Ops, SparseCore 0:
  98.1 42.3 reduce-scatter.1
  142.6 44.1 all-gather.1
where the time goes:
time: 286 us
  waiting for transfers between devices  155 us (54%)
  blocking collectives  84.5 us (30%)
  between operations  13.6 us (5%)
  local copies, waits for them, and re-layouts  10.6 us (4%)
  starting transfers between devices  10.4 us (4%)
  matrix products  7.4 us (3%)
  other arithmetic  4.12 us (1%)
    all_to_all x1, blocking collectives, on_device(): lax.all_to_all(rebuilt, 'theta', split_axis=3, concat_axis=3, tiled=True)  84.5 us
    all_to_all x1, waiting for transfers between devices, on_device(): lax.all_to_all(fields, 'theta', split_axis=3, concat_axis=3, tiled=True)  68.9 us
    all_gather x1, waiting for transfers between devices, spectral(): piece = lax.all_gather(masked, 'phi', axis=0, tiled=True)  44.4 us
    reduce_scatter x1, waiting for transfers between devices, spectral(): lax.psum_scatter(out.reshape(share_rows * lax.axis_size('phi'), groups *...  42.2 us
    all_to_all x1, starting transfers between devices, on_device(): lax.all_to_all(fields, 'theta', split_axis=3, concat_axis=3, tiled=True)  10.4 us
  transfers between devices with their start and end apart: 3, of which 3 were waited for; matrix products, arithmetic and copies ran while one was open for 1% of the time, Pallas kernels for 0%

commit v1 on v0

--- a/solution.py
+++ b/solution.py
@@ -5,6 +5,9 @@
 from jax.sharding import PartitionSpec as P
 
 KMAX = 384
+process_the_joints = lambda dim_at, x0: jnp.concatenate(
+    lax.all_to_all(jnp.stack([x0 for _ in range(lax.axis_size("phi"))]), "phi", 0, 0), dim_at
+)
 
 
 def tables(offset, span_rows, points, mode_count):
@@ -42,7 +45,7 @@
     share_index = phi_index * share_rows + jnp.arange(share_rows, dtype=jnp.int32)
     keep = (share_index % KMAX)[:, None] < line_counts[None, :]
     masked = jnp.where(keep, share, 0.0)
-    piece = lax.all_gather(masked, "phi", axis=0, tiled=True)
+    piece = process_the_joints(0, masked)
     stacked = piece.reshape(piece.shape[0], groups, rows_here)
     result = jnp.einsum(
         "kp,kgr->gpr", backward, stacked, precision=highest, preferred_element_type=jnp.float32

time: 286 us -> 306 us (1.070)
  waiting for transfers between devices: 155 us -> 164 us
  starting transfers between devices: 10.4 us -> 15.7 us
  local copies, waits for them, and re-layouts: 10.6 us -> 14.7 us
    all_to_all x0 -> x1, waiting for transfers between devices: none -> 52.9 us  [lax.all_to_all(jnp.stack([x0 for _ in range(lax.axis_size('phi'))]), 'phi...]
    all_gather x1 -> x0, waiting for transfers between devices: 44.4 us -> none  [spectral(): piece = lax.all_gather(masked, 'phi', axis=0, tiled=True)]
    all_to_all x0 -> x1, starting transfers between devices: none -> 5.34 us  [lax.all_to_all(jnp.stack([x0 for _ in range(lax.axis_size('phi'))]), 'phi...]
    another operation x0 -> x2, local copies, waits for them, and re-layouts: none -> 3.64 us  [the longest x1 2.04 us: spectral(): stacked = piece.reshape(piece.shape[0], groups, rows_here)]
where the time goes in v1:
time: 306 us; the launch traced here: 305 us
  waiting for transfers between devices  164 us (54%)
  blocking collectives  85 us (28%)
  starting transfers between devices  15.7 us (5%)
  local copies, waits for them, and re-layouts  14.7 us (5%)
  between operations  13.5 us (4%)
  matrix products  9.06 us (3%)
  other arithmetic  3.41 us (1%)
    all_to_all x1, blocking collectives, on_device(): lax.all_to_all(rebuilt, 'theta', split_axis=3, concat_axis=3, tiled=True)  85 us
    all_to_all x1, waiting for transfers between devices, on_device(): lax.all_to_all(fields, 'theta', split_axis=3, concat_axis=3, tiled=True)  68.9 us
    all_to_all x1, waiting for transfers between devices, lax.all_to_all(jnp.stack([x0 for _ in range(lax.axis_size('phi'))]), 'phi...  52.9 us
    reduce_scatter x1, waiting for transfers between devices, spectral(): lax.psum_scatter(out.reshape(share_rows * lax.axis_size('phi'), groups *...  42 us
    all_to_all x1, starting transfers between devices, on_device(): lax.all_to_all(fields, 'theta', split_axis=3, concat_axis=3, tiled=True)  10.4 us
  transfers between devices with their start and end apart: 3, of which 3 were waited for; matrix products, arithmetic and copies ran while one was open for 1% of the time, Pallas kernels for 0%

profile of v1, /device:TPU:1, one launch (start us, length us, event | category | flops | bytes accessed | tf_op | source)
XLA Modules:
  0.0 305.2 jit_solution(6784652926554864327)
XLA Ops:
  6.5 0.0 copy-start
  6.5 3.6 %copy.26 = f32[8,3,192,128]{2,0,1,3:T(8,128)} copy(f32[8,3,192,128]{3,2,1,0:T(8,128)} %param.2) | data formatting | bytes 4718592 | tf_op args[0]
  10.1 10.4 %all-to-all-start = ((f32[8,3,192,128]{2,0,1,3:T(8,128)}), f32[8,3,192,128]{2,0,1,3:T(8,128)S(1)}, u32[]{:S(2)}, u32[]{:S(2)}) async-start(f32[8,3,192,128]{2,0,1,3:T(8,128)} %copy.26), calls=%async_computation | async-start | bytes 6291456 | tf_op jit(solution)/shard_map/all_to_all | solution.py:64
  20.5 0.0 reduce-scatter.2.cloned.1.call-start
  20.5 2.1 fusion.10
  22.6 68.9 %all-to-all-done = f32[8,3,192,128]{2,0,1,3:T(8,128)S(1)} async-done(((f32[8,3,192,128]{2,0,1,3:T(8,128)}), f32[8,3,192,128]{2,0,1,3:T(8,128)S(1)}, u32[]{:S(2)}, u32[]{:S(2)}) %all-to-all-start) | async-done | bytes 2359328 | tf_op jit(solution)/shard_map/all_to_all | solution.py:64
  91.5 0.0 copy-start.1
  91.5 0.0 copy-start.2
  91.5 0.1 fusion.14
  91.5 0.1 copy.27
  91.7 0.1 copy.28
  91.8 0.1 pad_maximum_fusion.1
  91.9 0.7 copy-done.2
  92.6 5.4 %fusion.3 = f32[768,768]{1,0:T(8,128)} fusion(f32[768,192]{1,0:T(8,128)S(1)} %bitcast.17, f32[192,384]{1,0:T(8,128)S(1)} %copy-done.2, f32[192,384]{1,0:T(8,128)S(1)} %get-tuple-element.9), kind=kOutput, calls=%fused_computation.6 | convolution fusion | flops 1359101952 | bytes 3538944 | tf_op jit(solution)/shard_map/pk,gpr->kgr/dot_general | solution.py:36
  98.0 0.0 reduce-scatter.2.cloned.1.call-update
  98.0 0.0 copy-done
  98.0 0.1 constant_dynamic-slice_fusion
  98.1 0.1 broadcast_in_dim.23
  98.2 0.1 lt.33
  98.3 42.0 %reduce-scatter.2.cloned.1.call-done = f32[96,768]{1,0:T(8,128)} async-done(((f32[768,768]{1,0:T(8,128)}), f32[96,768]{1,0:T(8,128)}) %reduce-scatter.2.cloned.1.call-update) | async-done | bytes 294928 | tf_op jit(solution)/shard_map/reduce_scatter | solution.py:39
  140.3 1.0 compare_select_fusion
  141.3 1.6 stack.2
  142.9 5.3 %all-to-all-start.1 = ((f32[8,96,768]{2,1,0:T(8,128)}), f32[8,96,768]{2,1,0:T(8,128)}, u32[]{:S(2)}, u32[]{:S(2)}) async-start(f32[8,96,768]{2,1,0:T(8,128)} %stack.2), calls=%async_computation.2 | async-start | bytes 4718592 | tf_op jit(solution)/shard_map/all_to_all | solution.py:9
  148.3 0.0 copy-done.1
  148.3 52.9 %all-to-all-done.1 = f32[8,96,768]{2,1,0:T(8,128)} async-done(((f32[8,96,768]{2,1,0:T(8,128)}), f32[8,96,768]{2,1,0:T(8,128)}, u32[]{:S(2)}, u32[]{:S(2)}) %all-to-all-start.1) | async-done | bytes 2359328 | tf_op jit(solution)/shard_map/all_to_all | solution.py:9
  201.2 2.5 copy.29
  203.7 2.0 reshape_reshape.3
  205.7 3.7 %fusion = f32[24,32,192]{2,1,0:T(8,128)S(1)} fusion(f32[768,24,32]{0,2,1:T(8,128)} %reshape_reshape.3, f32[192,384]{1,0:T(8,128)} %get-tuple-element.10, f32[192,384]{1,0:T(8,128)S(1)} %get-tuple-element.9, f32[768]{0:T(1024)S(1)} %pad_maximum_fusion.5), kind=kOutput, calls=%fused_computation.3 | convolution fusion | flops 1359249408 | bytes 3542016 | tf_op jit(solution)/shard_map/kp,kgr->gpr/dot_general | solution.py:50
  209.4 0.0 slice-start
  209.4 0.1 fusion.15
  209.5 0.2 copy.33
  209.7 0.2 copy.34
  210.0 1.1 slice-done
  211.1 0.2 pad_maximum_fusion
  211.3 85.0 %all_to_all.15 = f32[8,3,192,128]{2,0,1,3:T(8,128)S(1)} all-to-all(f32[8,3,192,128]{2,0,1,3:T(8,128)S(1)} %pad_maximum_fusion), channel_id=1, replica_groups=mesh['phi'=8,'theta'=16,'row'=4] {'theta'}, dimensions={3} | all-to-all | bytes 4718592 | tf_op jit(solution)/shard_map/all_to_all | solution.py:82
  296.2 2.1 copy.32
  (5 shorter events, 0.0 us)
Async XLA Ops:
  6.5 91.5 %copy-start = (s32[512]{0:T(512)S(1)}, s32[512]{0:T(512)}, u32[]{:S(2)}) copy-start(s32[512]{0:T(512)} %param.3) | copy-start | bytes 6148
  10.1 81.4 %all-to-all-start = ((f32[8,3,192,128]{2,0,1,3:T(8,128)}), f32[8,3,192,128]{2,0,1,3:T(8,128)S(1)}, u32[]{:S(2)}, u32[]{:S(2)}) async-start(f32[8,3,192,128]{2,0,1,3:T(8,128)} %copy.26), calls=%async_computation | async-start | bytes 6291456 | tf_op jit(solution)/shard_map/all_to_all | solution.py:64
  20.5 119.8 %reduce-scatter.2.cloned.1.call-start = ((), (), s32[]{:S(2)}) async-start(), calls=%async_computation.4 | async-start | bytes 2654208 | tf_op jit(solution)/shard_map/reduce_scatter | solution.py:39
  91.5 56.9 %copy-start.1 = (f32[8,3,192,128]{2,0,1,3:T(8,128)}, f32[8,3,192,128]{2,0,1,3:T(8,128)S(1)}, u32[]{:S(2)}) copy-start(f32[8,3,192,128]{2,0,1,3:T(8,128)S(1)} %all-to-all-done) | copy-start | bytes 7077892
  91.5 1.2 copy-start.2
  142.9 58.2 %all-to-all-start.1 = ((f32[8,96,768]{2,1,0:T(8,128)}), f32[8,96,768]{2,1,0:T(8,128)}, u32[]{:S(2)}, u32[]{:S(2)}) async-start(f32[8,96,768]{2,1,0:T(8,128)} %stack.2), calls=%async_computation.2 | async-start | bytes 4718592 | tf_op jit(solution)/shard_map/all_to_all | solution.py:9
  209.4 1.7 slice-start
Sparse Core Ops, SparseCore 0:
  98.1 42.1 reduce-scatter.1
